TPU v7x, 768 devices: a whole 4x8x12 slice. The times are simulated.
768 devices in a mesh: grp: 96 (over z, y), blk: 8 (over x, core).
Axes of the slice: x: 4, y: 8, z: 12, core: 2. Of those that a mesh axis runs over, the one named last changes fastest.
Arguments:
- source: bfloat16 [786432, 256], P(('grp', 'blk')), may hold values from -6 to 6
- send_ids: int32 [768, 16], P(('grp', 'blk')), may hold values from 0 to 15
- send_counts: int32 [768, 8], P(('grp', 'blk')), may hold values from 1 to 2, as said below
- tile_slot: int32 [768, 128], P(('grp', 'blk')), may hold values from 0 to 15, as said below
- tile_target: int32 [768, 128], P(('grp', 'blk')), may hold values from 0 to 63, as said below
- tile_weights: bfloat16 [98304, 4096], P(('grp', 'blk')), may hold values from 0 to 0.0625
Outputs:
- remapped: float32 [1572864, 256], P(('grp', 'blk'))
Inputs may be any that keep to these rules, and one draw needn't show every extreme that they name: `send_counts`: every reader of every partition is sent at least one block, and each partition sends 2 blocks to some reader. `tile_slot`: each of the 8 * 2 receive slots is read by at least one tile of every partition. `tile_target`: each of the 64 partial target blocks is written by at least one tile of every partition.
All inputs are finite; a program needn't handle non-finite values.
Results may differ from a plain program's by a relative error of at most 0.0003.
Values may be sent and summed in bfloat16 or wider, within the bound.
A program may use at most 32 MiB of HBM per device.

v0:
```python
import jax
import jax.numpy as jnp
from jax import lax
from jax.sharding import PartitionSpec as P

COLS = 256
BLOCK = 64
TB = 32
EB = 16


def passed_along(shard, axis, by):
    count = lax.axis_size(axis)
    return lax.ppermute(shard, axis, [(i, (i + by) % count) for i in range(count)])


def body(source, send_ids, send_counts, tile_slot, tile_target, tile_weights):
    group_size = lax.axis_size("blk")
    own_index = lax.axis_index("blk")
    capacity = send_ids.shape[1] // group_size
    source_blocks = source.reshape(-1, BLOCK, COLS)
    slot_rank = jnp.arange(group_size * capacity, dtype=jnp.int32) % capacity
    all_ids, all_counts = (
        lax.all_gather(send_ids, "blk", axis=0, tiled=True),
        lax.all_gather(send_counts, "blk", axis=0, tiled=True),
    )
    block_ids = lax.dynamic_slice_in_dim(all_ids, own_index * capacity, capacity, 1)
    live_counts = lax.dynamic_slice_in_dim(all_counts, own_index, 1, 1)
    live_mask = (slot_rank.reshape(group_size, capacity) < live_counts).reshape(-1)
    sender_rank = jnp.arange(group_size * capacity, dtype=jnp.int32) // capacity
    global_ids = sender_rank * source_blocks.shape[0] + block_ids.reshape(-1)
    empty_slots = jnp.zeros((group_size * capacity, BLOCK, COLS), jnp.bfloat16)
    shard_blocks = lax.all_gather(source, "blk", axis=0, tiled=True).reshape(-1, BLOCK, COLS)
    count_here = shard_blocks.shape[0]
    wanted = (global_ids >= 0) & (global_ids < count_here) & live_mask
    picked = jnp.take(shard_blocks, jnp.clip(global_ids, 0, count_here - 1), axis=0)
    received = jnp.where(wanted[:, None, None], picked, empty_slots)
    tile_slots = tile_slot[0]
    tile_targets = tile_target[0]
    count_tiles = tile_slots.shape[0]
    weights = tile_weights.reshape(count_tiles, BLOCK, BLOCK)
    operands = jnp.take(received, tile_slots, axis=0)
    products = jnp.einsum("kij,kjc->kic", weights, operands, preferred_element_type=jnp.float32)
    segments = TB + 2 * EB
    onehot_table = (tile_targets[None, :] == jnp.arange(segments, dtype=jnp.int32)[:, None]).astype(
        jnp.float32
    )
    pieces = jnp.dot(
        onehot_table, products.reshape(count_tiles, BLOCK * COLS), precision=lax.Precision.HIGHEST
    )
    pieces = pieces.reshape(segments, BLOCK, COLS)
    lower_edge = pieces[:EB]
    middle = pieces[EB : EB + TB]
    upper_edge = pieces[EB + TB :]
    from_next = passed_along(lower_edge, ("grp", "blk"), -1)
    from_prior = passed_along(upper_edge, ("grp", "blk"), 1)
    assembled = jnp.concatenate(
        [middle[:EB] + from_prior, middle[EB : TB - EB], middle[TB - EB :] + from_next], axis=0
    )
    return assembled.reshape(TB * BLOCK, COLS)


def solution(mesh):
    return jax.shard_map(
        body,
        mesh=mesh,
        in_specs=(
            P(("grp", "blk"), None),
            P(("grp", "blk"), None),
            P(("grp", "blk"), None),
            P(("grp", "blk"), None),
            P(("grp", "blk"), None),
            P(("grp", "blk"), None),
        ),
        out_specs=P(("grp", "blk"), None),
        check_vma=False,
    )
```

profile of v0, /device:TPU:31, one launch (start us, length us, event | category | flops | bytes accessed | tf_op | source)
XLA Modules:
  0.0 109.9 jit_solution(9816836408256575367)
XLA Ops:
  6.5 0.0 copy-start.1
  6.5 0.0 all-gather.4.cloned.1.call-start
  6.5 0.7 all-gather.4.cloned.1.call-update
  7.3 8.0 %all-gather = s32[8,1,16]{2,1,0:T(1,128)S(1)} all-gather(s32[1,1,16]{2,1,0:T(1,128)} %bitcast.42), channel_id=1, replica_groups=mesh['grp'=96,'blk'=8] {'blk'}, dimensions={0}, use_global_device_ids=true | all-gather | bytes 576 | tf_op jit(solution)/shard_map/all_gather | solution.py:24
  15.3 0.5 broadcast.248
  15.8 0.7 fusion.15
  16.5 0.1 reshape.164
  16.6 0.1 reshape.166
  16.7 10.3 %all-gather.1 = s32[8,1,8]{2,1,0:T(1,128)S(1)} all-gather(s32[1,1,8]{2,1,0:T(1,128)} %bitcast.43), channel_id=1, replica_groups=mesh['grp'=96,'blk'=8] {'blk'}, dimensions={0}, use_global_device_ids=true | all-gather | bytes 288 | tf_op jit(solution)/shard_map/all_gather | solution.py:25
  27.0 0.3 dynamic-slice_reduce_fusion
  27.3 0.1 lt.79
  27.4 0.1 lt.80
  27.4 1.6 %copy.9 = bf16[128,4096]{0,1:T(8,128)(2,1)S(1)} copy(bf16[128,4096]{1,0:T(8,128)(2,1)} %param.11) | data formatting | bytes 2097152 | tf_op args[5]
  29.1 3.0 %copy.10 = bf16[128,64,64]{2,1,0:T(8,128)(2,1)S(1)} copy(bf16[128,64,64]{0,2,1:T(8,128)(2,1)S(1)} %bitcast.32) | data formatting | bytes 2097152 | tf_op jit(solution)/shard_map/reshape | solution.py:41
  32.1 0.0 copy-done.1
  32.2 22.8 %all-gather.4.cloned.1.call-done = bf16[8192,256]{1,0:T(8,128)(2,1)} async-done(((bf16[1024,256]{1,0:T(8,128)(2,1)}), bf16[8192,256]{1,0:T(8,128)(2,1)}) %all-gather.4.cloned.1.call-update) | async-done | bytes 4194320 | tf_op jit(solution)/shard_map/all_gather | solution.py:33
  55.0 2.8 %gather_fusion = bf16[16,64,256]{2,1,0:T(8,128)(2,1)S(1)} fusion(bf16[128,64,256]{2,1,0:T(8,128)(2,1)} %bitcast.39, s32[1024]{0:T(1024)S(1)} %pad_clamp_fusion.1), kind=kCustom, calls=%fused_computation | custom fusion | bytes 1048640 | tf_op jit(solution)/shard_map/jit(_take)/gather | solution.py:36
  57.7 0.1 select_select_fusion
  57.9 2.8 %gather_fusion.1 = bf16[128,64,256]{2,1,0:T(8,128)(2,1)} fusion(bf16[16,64,256]{2,1,0:T(8,128)(2,1)S(1)} %select_select_fusion, s32[1024]{0:T(1024)S(1)} %pad_clamp_fusion), kind=kCustom, calls=%fused_computation.1 | custom fusion | bytes 8389120 | tf_op jit(solution)/shard_map/jit(_take)/gather | solution.py:42
  60.6 3.5 %fusion = f32[128,256,64]{1,2,0:T(8,128)S(1)} fusion(bf16[128,64,64]{2,1,0:T(8,128)(2,1)S(1)} %copy.10, bf16[128,64,256]{2,1,0:T(8,128)(2,1)} %gather_fusion.1, pred[128]{0:T(512)(128)(4,1)S(1)} %compare_and_fusion.2), kind=kOutput, calls=%fused_computation.2 | convolution fusion | flops 270532608 | bytes 13631616 | tf_op jit(solution)/shard_map/kij,kjc->kic/dot_general | solution.py:43
  64.1 0.0 copy-start
  64.2 6.6 %copy.11 = f32[16,8,64,256]{3,1,2,0:T(8,128)S(1)} copy(f32[16,8,64,256]{3,2,1,0:T(8,128)S(1)} %bitcast.30) | data formatting | bytes 16777216
  70.8 0.0 copy-done
  70.8 3.8 %fusion.4 = f32[64,16384]{1,0:T(8,128)S(1)} fusion(f32[128,16384]{1,0:T(8,128)S(1)} %bitcast.31, s32[128]{0:T(128)S(1)} %bitcast.41), kind=kOutput, calls=%fused_computation.11 | convolution fusion | flops 1610620928 | bytes 12583424 | tf_op jit(solution)/shard_map/dot_general | solution.py:48
  74.6 0.5 fusion.16
  75.0 0.3 copy.13
  75.4 6.3 %collective-permute-start = (f32[16,64,256]{2,1,0:T(8,128)S(1)}, f32[16,64,256]{2,1,0:T(8,128)S(1)}, u32[]{:S(2)}, u32[]{:S(2)}) collective-permute-start(f32[16,64,256]{2,1,0:T(8,128)S(1)} %bitcast.38), channel_id=1, source_target_pairs={{0,1},{1,2},{2,3},{3,4},{4,5},{5,6},{6,7},{7,8},{8,9},{9,10},{10,1... | collective-permute-start | bytes 3145736 | tf_op jit(solution)/shard_map/ppermute | solution.py:14
  81.7 0.3 copy.15
  82.0 1.9 %collective-permute-start.1 = (f32[16,64,256]{2,1,0:T(8,128)S(1)}, f32[16,64,256]{2,1,0:T(8,128)S(1)}, u32[]{:S(2)}, u32[]{:S(2)}) collective-permute-start(f32[16,64,256]{2,1,0:T(8,128)S(1)} %bitcast.37), channel_id=1, source_target_pairs={{0,767},{1,0},{2,1},{3,2},{4,3},{5,4},{6,5},{7,6},{8,7},{9,8},{10,... | collective-permute-start | bytes 3145736 | tf_op jit(solution)/shard_map/ppermute | solution.py:14
  83.9 0.3 copy.12
  84.2 0.3 copy.14
  84.6 8.8 %collective-permute-done = f32[16,64,256]{2,1,0:T(8,128)S(1)} collective-permute-done((f32[16,64,256]{2,1,0:T(8,128)S(1)}, f32[16,64,256]{2,1,0:T(8,128)S(1)}, u32[]{:S(2)}, u32[]{:S(2)}) %collective-permute-start) | collective-permute-done | bytes 1048608 | tf_op jit(solution)/shard_map/ppermute | solution.py:14
  93.4 0.1 bitcast_add_fusion.1
  93.5 7.9 %collective-permute-done.1 = f32[16,64,256]{2,1,0:T(8,128)S(1)} collective-permute-done((f32[16,64,256]{2,1,0:T(8,128)S(1)}, f32[16,64,256]{2,1,0:T(8,128)S(1)}, u32[]{:S(2)}, u32[]{:S(2)}) %collective-permute-start.1) | collective-permute-done | bytes 1048608 | tf_op jit(solution)/shard_map/ppermute | solution.py:14
  101.4 0.1 bitcast_add_fusion
  101.6 1.5 %pad_maximum_fusion = f32[32,64,256]{2,1,0:T(8,128)} fusion(f32[16,64,256]{2,1,0:T(8,128)S(1)} %bitcast_add_fusion, f32[16,64,256]{2,1,0:T(8,128)S(1)} %bitcast_add_fusion.1), kind=kLoop, calls=%fused_computation.5 | loop fusion | flops 524288 | bytes 4194304 | tf_op jit(solution)/shard_map/concatenate | solution.py:57
  (7 shorter events, 0.1 us)
Async XLA Ops:
  6.5 25.5 %copy-start.1 = (s32[1,128]{1,0:T(1,128)S(1)}, s32[1,128]{1,0:T(1,128)}, u32[]{:S(2)}) copy-start(s32[1,128]{1,0:T(1,128)} %param.9) | copy-start | bytes 1540
  6.5 48.4 %all-gather.4.cloned.1.call-start = ((), (), s32[]{:S(2)}) async-start(), calls=%async_computation | async-start | bytes 4718592 | tf_op jit(solution)/shard_map/all_gather | solution.py:33
  64.1 6.6 %copy-start = (s32[1,128]{1,0:T(1,128)S(1)}, s32[1,128]{1,0:T(1,128)}, u32[]{:S(2)}) copy-start(s32[1,128]{1,0:T(1,128)} %param.10) | copy-start | bytes 1540
  75.4 18.0 %collective-permute-start = (f32[16,64,256]{2,1,0:T(8,128)S(1)}, f32[16,64,256]{2,1,0:T(8,128)S(1)}, u32[]{:S(2)}, u32[]{:S(2)}) collective-permute-start(f32[16,64,256]{2,1,0:T(8,128)S(1)} %bitcast.38), channel_id=1, source_target_pairs={{0,1},{1,2},{2,3},{3,4},{4,5},{5,6},{6,7},{7,8},{8,9},{9,10},{10,1... | collective-permute-start | bytes 3145736 | tf_op jit(solution)/shard_map/ppermute | solution.py:14
  82.0 19.4 %collective-permute-start.1 = (f32[16,64,256]{2,1,0:T(8,128)S(1)}, f32[16,64,256]{2,1,0:T(8,128)S(1)}, u32[]{:S(2)}, u32[]{:S(2)}) collective-permute-start(f32[16,64,256]{2,1,0:T(8,128)S(1)} %bitcast.37), channel_id=1, source_target_pairs={{0,767},{1,0},{2,1},{3,2},{4,3},{5,4},{6,5},{7,6},{8,7},{9,8},{10,... | collective-permute-start | bytes 3145736 | tf_op jit(solution)/shard_map/ppermute | solution.py:14
Sparse Core Ops, SparseCore 0:
  9.8 45.1 all-gather.3
where the time goes:
time: 110 us
  waiting for transfers between devices  40.2 us (37%)
  local copies, waits for them, and re-layouts  20.3 us (18%)
  blocking collectives  18.3 us (17%)
  between operations  13.6 us (12%)
  starting transfers between devices  8.22 us (7%)
  matrix products  7.28 us (7%)
  other arithmetic  1.99 us (2%)
    all_gather x1, waiting for transfers between devices, body(): lax.all_gather(source, 'blk', axis=0, tiled=True).reshape(-1, BLOCK, COLS)  22.8 us
    ppermute x2, waiting for transfers between devices, passed_along(): lax.ppermute(shard, axis, [(i, (i + by) % count) for i in range(count)])  16.7 us
    all_gather x1, blocking collectives, body(): lax.all_gather(send_counts, 'blk', axis=0, tiled=True)  10.3 us
    unnamed x10, local copies, waits for them, and re-layouts  9.49 us
    ppermute x2, starting transfers between devices, passed_along(): lax.ppermute(shard, axis, [(i, (i + by) % count) for i in range(count)])  8.22 us
    all_gather x1, blocking collectives, body(): lax.all_gather(send_ids, 'blk', axis=0, tiled=True)  8 us
    dot_general x1, matrix products, body(): jnp.dot(onehot_table, products.reshape(count_tiles, BLOCK * COLS), precis...  3.79 us
    dot_general x1, matrix products, body(): jnp.einsum('kij,kjc->kic', weights, operands, preferred_element_type=jnp....  3.49 us
  transfers between devices with their start and end apart: 3, of which 3 were waited for; matrix products, arithmetic and copies ran while one was open for 7% of the time, Pallas kernels for 0%

commit v1 on v0

v1 whole, which is shorter than its diff:
```python
import functools

import jax
import jax.numpy as jnp
from jax import lax
from jax.experimental import pallas as pl
from jax.experimental.pallas import tpu as pltpu
from jax.sharding import PartitionSpec as P

COLS = 256
BLOCK = 64
TB = 32
EB = 16
SEG = TB + 2 * EB
CHUNKS = 1
UNROLL = 8
ORDER = (4, 3, 5, 2, 6, 1, 7)
STEPS = 32766.0
MESH = pl.DeviceIdType.MESH


def tables(slot_ref, target_ref, table_ref):
    count = slot_ref.shape[1]
    key = (target_ref[...] + EB) % SEG
    across = jnp.broadcast_to(key, (count, count))
    down = across.T
    row = lax.broadcasted_iota(jnp.int32, (count, count), 0)
    col = lax.broadcasted_iota(jnp.int32, (count, count), 1)
    ahead = (down < across) | ((down == across) & (row < col))
    rank = jnp.sum(ahead.astype(jnp.int32), axis=0, keepdims=True)
    packed = lax.broadcasted_iota(jnp.int32, (1, count), 1) + 128 * slot_ref[...] + 2048 * key
    rank_down = jnp.broadcast_to(rank, (count, count)).T
    packed_down = jnp.broadcast_to(packed, (count, count)).T
    ordered = jnp.sum(jnp.where(rank_down == col, packed_down, 0), axis=0, keepdims=True)
    goal = ordered >> 11
    same = (goal == pltpu.roll(goal, 1, 1)) & (lax.broadcasted_iota(jnp.int32, (1, count), 1) > 0)
    table_ref[0:1, :] = ordered & 127
    table_ref[1:2, :] = (ordered >> 7) & 15
    table_ref[2:3, :] = same.astype(jnp.int32)
    upto = jnp.sum((down <= col).astype(jnp.int32), axis=0, keepdims=True)
    table_ref[3:4, :] = jnp.maximum(upto - 1, 0)


def kernel(
    groups, size,
    ids_ref, counts_ref, slot_ref, target_ref, source_hbm, weights_hbm, out_ref,
    source, flat, tiles, outgoing, received, sums, table, table_s,
    edge_out, scale_out, edge_in, scale_in,
    local_sem, send_sem, recv_sem, edge_send, edge_recv,
):
    group, me = lax.axis_index("grp"), lax.axis_index("blk")
    count = slot_ref.shape[1]
    width = COLS // CHUNKS
    cap = ids_ref.shape[1] // size
    after = ((group + (me + 1) // size) % groups, (me + 1) % size)
    before = ((group + groups - 1 + (me + size - 1) // size) % groups, (me + size - 1) % size)

    barrier = pltpu.get_barrier_semaphore()
    for k in range(1, size):
        pl.semaphore_signal(barrier, inc=1, device_id=(group, (me + k) % size), device_id_type=MESH)
    pl.semaphore_signal(barrier, inc=1, device_id=after, device_id_type=MESH)
    pl.semaphore_signal(barrier, inc=1, device_id=before, device_id_type=MESH)

    load_source = pltpu.make_async_copy(source_hbm, source, local_sem.at[0])
    load_weights = pltpu.make_async_copy(weights_hbm, flat, local_sem.at[1])
    load_source.start()
    load_weights.start()
    load_source.wait()

    sends = []
    for c in range(CHUNKS):
        columns = slice(c * width, (c + 1) * width)
        for k in (0,) + ORDER:
            reader = (me + k) % size
            live = counts_ref[0, reader]
            for j in range(cap):
                block = source[ids_ref[0, reader * cap + j], :, columns]
                kept = jnp.clip(live - j, 0, 1).astype(jnp.float32)
                block = block * jnp.full(block.shape, kept, jnp.float32).astype(block.dtype)
                if k == 0:
                    received[c, me * cap + j] = block
                else:
                    outgoing[c, k, j] = block
    pl.semaphore_wait(barrier, size + 1)
    for c in range(CHUNKS):
        sends.append({})
        for k in ORDER:
            copy = pltpu.make_async_remote_copy(
                src_ref=outgoing.at[c, k],
                dst_ref=received.at[c, pl.ds(me * cap, cap)],
                send_sem=send_sem.at[c, k],
                recv_sem=recv_sem.at[c, k],
                device_id=(group, (me + k) % size),
                device_id_type=MESH,
            )
            copy.start()
            sends[c][k] = copy

    tables(slot_ref, target_ref, table)
    fill = pltpu.make_async_copy(table, table_s, local_sem.at[2])
    fill.start()
    load_weights.wait()

    rows = tiles.reshape(count * BLOCK, 2 * BLOCK)

    @pl.loop(0, count // 16)
    def _(a):
        first = pl.multiple_of(a * 16, 16)
        for i in range(0, BLOCK, 2):
            pair = flat[pl.ds(first, 16), i * BLOCK : (i + 2) * BLOCK].astype(jnp.float32)
            rows[pl.ds(first * BLOCK + i, 16, stride=BLOCK), :] = pair
            rows[pl.ds(first * BLOCK + i + 1, 16, stride=BLOCK), :] = pltpu.roll(pair, BLOCK, 1)

    fill.wait()

    def send_edge(c, side):
        dest = after if side == 0 else before
        copies = []
        for n, (src, dst) in enumerate(((edge_out, edge_in), (scale_out, scale_in))):
            copy = pltpu.make_async_remote_copy(
                src_ref=src.at[c, side],
                dst_ref=dst.at[c, side],
                send_sem=edge_send.at[c, side, n],
                recv_sem=edge_recv.at[c, side, n],
                device_id=dest,
                device_id_type=MESH,
            )
            copy.start()
            copies.append(copy)
        return copies

    edges = []
    for c in range(CHUNKS):
        columns = slice(c * width, (c + 1) * width)
        for k in ORDER:
            sends[c][k].wait_recv()

        def run(step, total):
            for u in range(UNROLL):
                place = step * UNROLL + u
                block = received[c, table_s[1, place]]
                tile = tiles[table_s[0, place]][:, :BLOCK].astype(jnp.bfloat16)
                part = jnp.dot(tile, block, preferred_element_type=jnp.float32)
                total = part + total * table_s[2, place].astype(jnp.float32)
                sums[place] = total
            return total

        lax.fori_loop(0, count // UNROLL, run, jnp.zeros((BLOCK, width), jnp.float32))

        edges.append([])
        for side in range(2):

            @pl.loop(0, EB)
            def _(i):
                whole = sums[table_s[3, side * EB + i]]
                most = jnp.maximum(jnp.max(jnp.abs(whole), axis=0, keepdims=True), 1e-30)
                coded = jnp.round(whole * (STEPS / most))
                edge_out[c, side, i] = coded.astype(jnp.int32).astype(jnp.int16)
                scale_out[c, side, i] = most * (1.0 / STEPS)

            edges[c].append(send_edge(c, side))

        @pl.loop(0, TB)
        def _(i):
            out_ref[i, :, columns] = sums[table_s[3, 2 * EB + i]]

    for c in range(CHUNKS):
        columns = slice(c * width, (c + 1) * width)
        for side in range(2):
            for copy in edges[c][side]:
                copy.wait_recv()

            @pl.loop(0, EB)
            def _(i):
                part = edge_in[c, side, i].astype(jnp.int32).astype(jnp.float32) * scale_in[c, side, i]
                spot = i + (0 if side == 0 else TB - EB)
                out_ref[spot, :, columns] = out_ref[spot, :, columns] + part

    for c in range(CHUNKS):
        for k in ORDER:
            sends[c][k].wait_send()
        for side in range(2):
            for copy in edges[c][side]:
                copy.wait_send()


def body(groups, size, source, send_ids, send_counts, tile_slot, tile_target, tile_weights):
    count = tile_weights.shape[0]
    cap = send_ids.shape[1] // size
    width = COLS // CHUNKS
    blocks = source.shape[0] // BLOCK
    smem = pl.BlockSpec(memory_space=pltpu.SMEM)
    vmem = pl.BlockSpec(memory_space=pltpu.VMEM)
    hbm = pl.BlockSpec(memory_space=pl.ANY)
    dma = pltpu.SemaphoreType.DMA
    out = pl.pallas_call(
        functools.partial(kernel, groups, size),
        out_shape=jax.ShapeDtypeStruct((TB, BLOCK, COLS), jnp.float32),
        in_specs=[smem, smem, vmem, vmem, hbm, hbm],
        out_specs=vmem,
        scratch_shapes=[
            pltpu.VMEM((blocks, BLOCK, COLS), jnp.bfloat16),
            pltpu.VMEM((count, BLOCK * BLOCK), jnp.bfloat16),
            pltpu.VMEM((count, BLOCK, 2 * BLOCK), jnp.float32),
            pltpu.VMEM((CHUNKS, size, cap, BLOCK, width), jnp.bfloat16),
            pltpu.VMEM((CHUNKS, size * cap, BLOCK, width), jnp.bfloat16),
            pltpu.VMEM((count, BLOCK, width), jnp.float32),
            pltpu.VMEM((8, count), jnp.int32),
            pltpu.SMEM((8, count), jnp.int32),
            pltpu.VMEM((CHUNKS, 2, EB, BLOCK, width), jnp.int16),
            pltpu.VMEM((CHUNKS, 2, EB, 1, width), jnp.float32),
            pltpu.VMEM((CHUNKS, 2, EB, BLOCK, width), jnp.int16),
            pltpu.VMEM((CHUNKS, 2, EB, 1, width), jnp.float32),
            dma((3,)),
            dma((CHUNKS, size)),
            dma((CHUNKS, size)),
            dma((CHUNKS, 2, 2)),
            dma((CHUNKS, 2, 2)),
        ],
        compiler_params=pltpu.CompilerParams(
            collective_id=0, has_side_effects=True, vmem_limit_bytes=48 << 20
        ),
    )(send_ids, send_counts, tile_slot, tile_target, source.reshape(blocks, BLOCK, COLS), tile_weights)
    return out.reshape(TB * BLOCK, COLS)


def solution(mesh):
    sizes = (mesh.shape["grp"], mesh.shape["blk"])
    return jax.shard_map(
        functools.partial(body, *sizes),
        mesh=mesh,
        in_specs=(P(("grp", "blk"), None),) * 6,
        out_specs=P(("grp", "blk"), None),
        check_vma=False,
    )
```

time: 110 us -> 46.9 us (0.43)
  the two profiles are of different devices: /device:TPU:31 before, /device:TPU:8 now
where the time goes in v1:
time: 46.9 us; the launch traced here: 46.6 us
  Pallas kernels  40.4 us (86%)
  local copies, waits for them, and re-layouts  6.21 us (13%)
    pallas_call x1, Pallas kernels, body(): pl.pallas_call(functools.partial(kernel, groups, size), out_shape=jax.Sha...  40.4 us
    unnamed x13, local copies, waits for them, and re-layouts  6.21 us

profile of v1, /device:TPU:8, one launch (start us, length us, event | category | flops | bytes accessed | tf_op | source)
XLA Modules:
  0.0 46.6 jit_solution(12974200358595766778)
XLA Ops:
  0.0 0.0 copy-start
  0.0 1.2 %copy-done = bf16[128,4096]{1,0:T(8,128)(2,1)S(1)} copy-done((bf16[128,4096]{1,0:T(8,128)(2,1)S(1)}, bf16[128,4096]{1,0:T(8,128)(2,1)}, u32[]{:S(2)}) %copy-start) | copy-done | bytes 1048600
  1.2 0.0 copy-start.1
  1.2 1.0 %copy-done.1 = bf16[1024,256]{1,0:T(8,128)(2,1)S(1)} copy-done((bf16[1024,256]{1,0:T(8,128)(2,1)S(1)}, bf16[1024,256]{1,0:T(8,128)(2,1)}, u32[]{:S(2)}) %copy-start.1) | copy-done | bytes 524312
  2.3 0.0 copy-start.2
  2.3 0.7 %copy-done.2 = s32[1,16]{1,0:T(1,128)S(1)} copy-done((s32[1,16]{1,0:T(1,128)S(1)}, s32[1,16]{1,0:T(1,128)}, u32[]{:S(2)}) %copy-start.2) | copy-done | bytes 88
  2.9 0.0 copy-start.3
  2.9 0.7 %copy-done.3 = s32[1,8]{1,0:T(1,128)S(1)} copy-done((s32[1,8]{1,0:T(1,128)S(1)}, s32[1,8]{1,0:T(1,128)}, u32[]{:S(2)}) %copy-start.3) | copy-done | bytes 56
  3.6 0.0 copy-start.4
  3.6 0.7 %copy-done.4 = s32[1,128]{1,0:T(1,128)S(1)} copy-done((s32[1,128]{1,0:T(1,128)S(1)}, s32[1,128]{1,0:T(1,128)}, u32[]{:S(2)}) %copy-start.4) | copy-done | bytes 536
  4.2 0.0 copy-start.5
  4.2 0.7 %copy-done.5 = s32[1,128]{1,0:T(1,128)S(1)} copy-done((s32[1,128]{1,0:T(1,128)S(1)}, s32[1,128]{1,0:T(1,128)}, u32[]{:S(2)}) %copy-start.5) | copy-done | bytes 536
  4.9 40.4 %shard_map.64 = f32[32,64,256]{2,1,0:T(8,128)S(1)} custom-call(s32[1,16]{1,0:T(1,128)S(1)} %copy-done.2, s32[1,8]{1,0:T(1,128)S(1)} %copy-done.3, s32[1,128]{1,0:T(1,128)S(1)} %copy-done.4, s32[1,128]{1,0:T(1,128)S(1)} %copy-done.5, bf16[16,64,256]{2,1,0:T(8,128)(2,1)S(1)} %bitcast.3, bf16[128,4096]{1,0:T(8,128)(2,1)S(1)} %copy-done), custom_call_target="tpu_custom_call" | custom-call | tf_op jit(solution)/shard_map/pallas_call | solution.py:196
  45.3 1.3 %copy.8 = f32[2048,256]{1,0:T(8,128)} copy(f32[2048,256]{1,0:T(8,128)S(1)} %bitcast.2) | data formatting | bytes 4194304
Async XLA Ops:
  0.0 1.2 %copy-start = (bf16[128,4096]{1,0:T(8,128)(2,1)S(1)}, bf16[128,4096]{1,0:T(8,128)(2,1)}, u32[]{:S(2)}) copy-start(bf16[128,4096]{1,0:T(8,128)(2,1)} %weights_hbm.1) | copy-start | bytes 3145732
  1.2 1.0 %copy-start.1 = (bf16[1024,256]{1,0:T(8,128)(2,1)S(1)}, bf16[1024,256]{1,0:T(8,128)(2,1)}, u32[]{:S(2)}) copy-start(bf16[1024,256]{1,0:T(8,128)(2,1)} %param.6) | copy-start | bytes 1572868
  2.3 0.7 %copy-start.2 = (s32[1,16]{1,0:T(1,128)S(1)}, s32[1,16]{1,0:T(1,128)}, u32[]{:S(2)}) copy-start(s32[1,16]{1,0:T(1,128)} %ids_ref.1) | copy-start | bytes 196
  2.9 0.7 %copy-start.3 = (s32[1,8]{1,0:T(1,128)S(1)}, s32[1,8]{1,0:T(1,128)}, u32[]{:S(2)}) copy-start(s32[1,8]{1,0:T(1,128)} %counts_ref.1) | copy-start | bytes 100
  3.6 0.7 %copy-start.4 = (s32[1,128]{1,0:T(1,128)S(1)}, s32[1,128]{1,0:T(1,128)}, u32[]{:S(2)}) copy-start(s32[1,128]{1,0:T(1,128)} %slot_ref.1) | copy-start | bytes 1540
  4.2 0.7 %copy-start.5 = (s32[1,128]{1,0:T(1,128)S(1)}, s32[1,128]{1,0:T(1,128)}, u32[]{:S(2)}) copy-start(s32[1,128]{1,0:T(1,128)} %target_ref.1) | copy-start | bytes 1540

commit v2 on v1

--- a/solution.py
+++ b/solution.py
@@ -13,9 +13,11 @@
 EB = 16
 SEG = TB + 2 * EB
 CHUNKS = 1
-UNROLL = 8
+UNROLL = 32
 ORDER = (4, 3, 5, 2, 6, 1, 7)
 STEPS = 32766.0
+PIECE = 4
+PIECES = [(piece, side) for piece in range(EB // PIECE) for side in range(2)]
 MESH = pl.DeviceIdType.MESH
 
 
@@ -43,15 +45,15 @@
 
 def kernel(
     groups, size,
-    ids_ref, counts_ref, slot_ref, target_ref, source_hbm, weights_hbm, out_ref,
-    source, flat, tiles, outgoing, received, sums, table, table_s,
+    ids_hbm, counts_hbm, slot_hbm, target_hbm, source_hbm, weights_hbm, out_ref,
+    ids_ref, counts_ref, slot_ref, target_ref, source, flat, tiles, outgoing, received, sums, table, table_s,
     edge_out, scale_out, edge_in, scale_in,
     local_sem, send_sem, recv_sem, edge_send, edge_recv,
 ):
     group, me = lax.axis_index("grp"), lax.axis_index("blk")
-    count = slot_ref.shape[1]
+    count = slot_hbm.shape[1]
     width = COLS // CHUNKS
-    cap = ids_ref.shape[1] // size
+    cap = ids_hbm.shape[1] // size
     after = ((group + (me + 1) // size) % groups, (me + 1) % size)
     before = ((group + groups - 1 + (me + size - 1) // size) % groups, (me + size - 1) % size)
 
@@ -61,11 +63,15 @@
     pl.semaphore_signal(barrier, inc=1, device_id=after, device_id_type=MESH)
     pl.semaphore_signal(barrier, inc=1, device_id=before, device_id_type=MESH)
 
-    load_source = pltpu.make_async_copy(source_hbm, source, local_sem.at[0])
-    load_weights = pltpu.make_async_copy(weights_hbm, flat, local_sem.at[1])
-    load_source.start()
-    load_weights.start()
-    load_source.wait()
+    pairs = (
+        (ids_hbm, ids_ref), (counts_hbm, counts_ref), (source_hbm, source),
+        (slot_hbm, slot_ref), (target_hbm, target_ref), (weights_hbm, flat),
+    )
+    loads = [pltpu.make_async_copy(src, dst, local_sem.at[n]) for n, (src, dst) in enumerate(pairs)]
+    for load in loads:
+        load.start()
+    for load in loads[:3]:
+        load.wait()
 
     sends = []
     for c in range(CHUNKS):
@@ -96,10 +102,11 @@
             copy.start()
             sends[c][k] = copy
 
+    for load in loads[3:]:
+        load.wait()
     tables(slot_ref, target_ref, table)
-    fill = pltpu.make_async_copy(table, table_s, local_sem.at[2])
+    fill = pltpu.make_async_copy(table, table_s, local_sem.at[6])
     fill.start()
-    load_weights.wait()
 
     rows = tiles.reshape(count * BLOCK, 2 * BLOCK)
 
@@ -113,21 +120,19 @@
 
     fill.wait()
 
-    def send_edge(c, side):
-        dest = after if side == 0 else before
-        copies = []
-        for n, (src, dst) in enumerate(((edge_out, edge_in), (scale_out, scale_in))):
-            copy = pltpu.make_async_remote_copy(
-                src_ref=src.at[c, side],
-                dst_ref=dst.at[c, side],
-                send_sem=edge_send.at[c, side, n],
-                recv_sem=edge_recv.at[c, side, n],
-                device_id=dest,
+    def edge_copies(c, side, piece):
+        part = pl.ds(piece * PIECE, PIECE)
+        return [
+            pltpu.make_async_remote_copy(
+                src_ref=src.at[c, side, part],
+                dst_ref=dst.at[c, side, part],
+                send_sem=edge_send.at[c, side, piece, n],
+                recv_sem=edge_recv.at[c, side, piece, n],
+                device_id=(after, before)[side],
                 device_id_type=MESH,
             )
-            copy.start()
-            copies.append(copy)
-        return copies
+            for n, (src, dst) in enumerate(((scale_out, scale_in), (edge_out, edge_in)))
+        ]
 
     edges = []
     for c in range(CHUNKS):
@@ -147,10 +152,10 @@
 
         lax.fori_loop(0, count // UNROLL, run, jnp.zeros((BLOCK, width), jnp.float32))
 
-        edges.append([])
-        for side in range(2):
-
-            @pl.loop(0, EB)
+        edges.append({})
+        for piece, side in PIECES:
+
+            @pl.loop(piece * PIECE, (piece + 1) * PIECE)
             def _(i):
                 whole = sums[table_s[3, side * EB + i]]
                 most = jnp.maximum(jnp.max(jnp.abs(whole), axis=0, keepdims=True), 1e-30)
@@ -158,7 +163,9 @@
                 edge_out[c, side, i] = coded.astype(jnp.int32).astype(jnp.int16)
                 scale_out[c, side, i] = most * (1.0 / STEPS)
 
-            edges[c].append(send_edge(c, side))
+            edges[c][piece, side] = edge_copies(c, side, piece)
+            for copy in edges[c][piece, side]:
+                copy.start()
 
         @pl.loop(0, TB)
         def _(i):
@@ -166,11 +173,11 @@
 
     for c in range(CHUNKS):
         columns = slice(c * width, (c + 1) * width)
-        for side in range(2):
-            for copy in edges[c][side]:
+        for piece, side in PIECES:
+            for copy in edges[c][piece, side]:
                 copy.wait_recv()
 
-            @pl.loop(0, EB)
+            @pl.loop(piece * PIECE, (piece + 1) * PIECE)
             def _(i):
                 part = edge_in[c, side, i].astype(jnp.int32).astype(jnp.float32) * scale_in[c, side, i]
                 spot = i + (0 if side == 0 else TB - EB)
@@ -179,8 +186,8 @@
     for c in range(CHUNKS):
         for k in ORDER:
             sends[c][k].wait_send()
-        for side in range(2):
-            for copy in edges[c][side]:
+        for copies in edges[c].values():
+            for copy in copies:
                 copy.wait_send()
 
 
@@ -189,16 +196,23 @@
     cap = send_ids.shape[1] // size
     width = COLS // CHUNKS
     blocks = source.shape[0] // BLOCK
-    smem = pl.BlockSpec(memory_space=pltpu.SMEM)
     vmem = pl.BlockSpec(memory_space=pltpu.VMEM)
-    hbm = pl.BlockSpec(memory_space=pl.ANY)
+    hbm = pl.BlockSpec(memory_space=pltpu.HBM)
     dma = pltpu.SemaphoreType.DMA
+    operands = (
+        send_ids, send_counts, tile_slot, tile_target,
+        source.reshape(blocks, BLOCK, COLS), tile_weights,
+    )
     out = pl.pallas_call(
         functools.partial(kernel, groups, size),
         out_shape=jax.ShapeDtypeStruct((TB, BLOCK, COLS), jnp.float32),
-        in_specs=[smem, smem, vmem, vmem, hbm, hbm],
+        in_specs=[hbm] * 6,
         out_specs=vmem,
         scratch_shapes=[
+            pltpu.SMEM(send_ids.shape, jnp.int32),
+            pltpu.SMEM(send_counts.shape, jnp.int32),
+            pltpu.VMEM(tile_slot.shape, jnp.int32),
+            pltpu.VMEM(tile_target.shape, jnp.int32),
             pltpu.VMEM((blocks, BLOCK, COLS), jnp.bfloat16),
             pltpu.VMEM((count, BLOCK * BLOCK), jnp.bfloat16),
             pltpu.VMEM((count, BLOCK, 2 * BLOCK), jnp.float32),
@@ -211,16 +225,16 @@
             pltpu.VMEM((CHUNKS, 2, EB, 1, width), jnp.float32),
             pltpu.VMEM((CHUNKS, 2, EB, BLOCK, width), jnp.int16),
             pltpu.VMEM((CHUNKS, 2, EB, 1, width), jnp.float32),
-            dma((3,)),
+            dma((7,)),
             dma((CHUNKS, size)),
             dma((CHUNKS, size)),
-            dma((CHUNKS, 2, 2)),
-            dma((CHUNKS, 2, 2)),
+            dma((CHUNKS, 2, EB // PIECE, 2)),
+            dma((CHUNKS, 2, EB // PIECE, 2)),
         ],
         compiler_params=pltpu.CompilerParams(
             collective_id=0, has_side_effects=True, vmem_limit_bytes=48 << 20
         ),
-    )(send_ids, send_counts, tile_slot, tile_target, source.reshape(blocks, BLOCK, COLS), tile_weights)
+    )(*(pltpu.with_memory_space_constraint(x, pltpu.HBM) for x in operands))
     return out.reshape(TB * BLOCK, COLS)
 
 

time: 46.9 us -> 37.2 us (0.79)
  the two profiles are of different devices: /device:TPU:8 before, /device:TPU:1 now
where the time goes in v2:
time: 37.2 us; the launch traced here: 37 us
  Pallas kernels  35.7 us (96%)
  local copies, waits for them, and re-layouts  1.32 us (4%)
    pallas_call x1, Pallas kernels, body(): pl.pallas_call(functools.partial(kernel, groups, size), out_shape=jax.Sha...  35.7 us
    unnamed x1, local copies, waits for them, and re-layouts  1.32 us

profile of v2, /device:TPU:1, one launch (start us, length us, event | category | flops | bytes accessed | tf_op | source)
XLA Modules:
  0.0 37.0 jit_solution(14169892343587745218)
XLA Ops:
  0.0 35.7 %shard_map.64 = f32[32,64,256]{2,1,0:T(8,128)S(1)} custom-call(s32[1,16]{1,0:T(1,128)} %ids_hbm.1, s32[1,8]{1,0:T(1,128)} %counts_hbm.1, s32[1,128]{1,0:T(1,128)} %slot_hbm.1, s32[1,128]{1,0:T(1,128)} %target_hbm.1, bf16[16,64,256]{2,1,0:T(8,128)(2,1)} %bitcast.3, bf16[128,4096]{1,0:T(8,128)(2,1)} %weights_hbm.1), custom_call_target="tpu_custom_call" | custom-call | tf_op jit(solution)/shard_map/pallas_call | solution.py:206
  35.7 1.3 %copy.8 = f32[2048,256]{1,0:T(8,128)} copy(f32[2048,256]{1,0:T(8,128)S(1)} %bitcast.2) | data formatting | bytes 4194304

commit v3 on v2

--- a/solution.py
+++ b/solution.py
@@ -9,10 +9,11 @@
 
 COLS = 256
 BLOCK = 64
+HALF = BLOCK // 2
 TB = 32
 EB = 16
 SEG = TB + 2 * EB
-CHUNKS = 1
+CHUNKS = 2
 UNROLL = 32
 ORDER = (4, 3, 5, 2, 6, 1, 7)
 STEPS = 32766.0
@@ -46,7 +47,7 @@
 def kernel(
     groups, size,
     ids_hbm, counts_hbm, slot_hbm, target_hbm, source_hbm, weights_hbm, out_ref,
-    ids_ref, counts_ref, slot_ref, target_ref, source, flat, tiles, outgoing, received, sums, table, table_s,
+    ids_ref, counts_ref, slot_ref, target_ref, source, flat, tiles, outgoing, received, twice, sums, table, table_s,
     edge_out, scale_out, edge_in, scale_in,
     local_sem, send_sem, recv_sem, edge_send, edge_recv,
 ):
@@ -73,25 +74,22 @@
     for load in loads[:3]:
         load.wait()
 
-    sends = []
-    for c in range(CHUNKS):
+    def pack(c):
         columns = slice(c * width, (c + 1) * width)
-        for k in (0,) + ORDER:
+
+        @pl.loop(0, size)
+        def _(k):
             reader = (me + k) % size
             live = counts_ref[0, reader]
             for j in range(cap):
                 block = source[ids_ref[0, reader * cap + j], :, columns]
                 kept = jnp.clip(live - j, 0, 1).astype(jnp.float32)
-                block = block * jnp.full(block.shape, kept, jnp.float32).astype(block.dtype)
-                if k == 0:
-                    received[c, me * cap + j] = block
-                else:
-                    outgoing[c, k, j] = block
-    pl.semaphore_wait(barrier, size + 1)
-    for c in range(CHUNKS):
-        sends.append({})
+                outgoing[c, k, j] = block * jnp.full(block.shape, kept, jnp.float32).astype(block.dtype)
+
+    def send(c):
+        copies = {}
         for k in ORDER:
-            copy = pltpu.make_async_remote_copy(
+            copies[k] = pltpu.make_async_remote_copy(
                 src_ref=outgoing.at[c, k],
                 dst_ref=received.at[c, pl.ds(me * cap, cap)],
                 send_sem=send_sem.at[c, k],
@@ -99,8 +97,15 @@
                 device_id=(group, (me + k) % size),
                 device_id_type=MESH,
             )
-            copy.start()
-            sends[c][k] = copy
+            copies[k].start()
+        for j in range(cap):
+            received[c, me * cap + j] = outgoing[c, 0, j]
+        return copies
+
+    pack(0)
+    pl.semaphore_wait(barrier, size + 1)
+    sends = [send(0)]
+    pack(1)
 
     for load in loads[3:]:
         load.wait()
@@ -108,16 +113,27 @@
     fill = pltpu.make_async_copy(table, table_s, local_sem.at[6])
     fill.start()
 
-    rows = tiles.reshape(count * BLOCK, 2 * BLOCK)
+    rows = tiles.reshape(count * HALF, 2 * BLOCK)
+    left = lax.broadcasted_iota(jnp.int32, (16, 2 * BLOCK), 1) < BLOCK
 
     @pl.loop(0, count // 16)
     def _(a):
         first = pl.multiple_of(a * 16, 16)
-        for i in range(0, BLOCK, 2):
-            pair = flat[pl.ds(first, 16), i * BLOCK : (i + 2) * BLOCK].astype(jnp.float32)
-            rows[pl.ds(first * BLOCK + i, 16, stride=BLOCK), :] = pair
-            rows[pl.ds(first * BLOCK + i + 1, 16, stride=BLOCK), :] = pltpu.roll(pair, BLOCK, 1)
-
+        for i in range(HALF // 2):
+            low, high = (
+                flat[pl.ds(first, 16), at * BLOCK : (at + 2) * BLOCK].astype(jnp.float32)
+                for at in (2 * i, HALF + 2 * i)
+            )
+            even = jnp.where(left, low, pltpu.roll(high, BLOCK, 1))
+            odd = jnp.where(left, pltpu.roll(low, BLOCK, 1), high)
+            rows[pl.ds(first * HALF + 2 * i, 16, stride=HALF), :] = even
+            rows[pl.ds(first * HALF + 2 * i + 1, 16, stride=HALF), :] = odd
+
+    @pl.loop(0, size * cap)
+    def _(slot):
+        twice[slot] = jnp.zeros(twice.shape[1:], twice.dtype)
+
+    sends.append(send(1))
     fill.wait()
 
     def edge_copies(c, side, piece):
@@ -136,28 +152,32 @@
 
     edges = []
     for c in range(CHUNKS):
-        columns = slice(c * width, (c + 1) * width)
         for k in ORDER:
             sends[c][k].wait_recv()
+
+        @pl.loop(0, size * cap)
+        def _(slot):
+            block = received[c, slot]
+            twice[slot, :BLOCK, :width] = block
+            twice[slot, BLOCK:, width:] = block
 
         def run(step, total):
             for u in range(UNROLL):
                 place = step * UNROLL + u
-                block = received[c, table_s[1, place]]
-                tile = tiles[table_s[0, place]][:, :BLOCK].astype(jnp.bfloat16)
-                part = jnp.dot(tile, block, preferred_element_type=jnp.float32)
+                tile = tiles[table_s[0, place]].astype(jnp.bfloat16)
+                part = jnp.dot(tile, twice[table_s[1, place]], preferred_element_type=jnp.float32)
                 total = part + total * table_s[2, place].astype(jnp.float32)
-                sums[place] = total
+                sums[c, place] = total
             return total
 
-        lax.fori_loop(0, count // UNROLL, run, jnp.zeros((BLOCK, width), jnp.float32))
+        lax.fori_loop(0, count // UNROLL, run, jnp.zeros((HALF, 2 * width), jnp.float32))
 
         edges.append({})
         for piece, side in PIECES:
 
             @pl.loop(piece * PIECE, (piece + 1) * PIECE)
             def _(i):
-                whole = sums[table_s[3, side * EB + i]]
+                whole = sums[c, table_s[3, side * EB + i]]
                 most = jnp.maximum(jnp.max(jnp.abs(whole), axis=0, keepdims=True), 1e-30)
                 coded = jnp.round(whole * (STEPS / most))
                 edge_out[c, side, i] = coded.astype(jnp.int32).astype(jnp.int16)
@@ -167,9 +187,14 @@
             for copy in edges[c][piece, side]:
                 copy.start()
 
+    for c in range(CHUNKS):
+        columns = slice(c * width, (c + 1) * width)
+
         @pl.loop(0, TB)
         def _(i):
-            out_ref[i, :, columns] = sums[table_s[3, 2 * EB + i]]
+            whole = sums[c, table_s[3, 2 * EB + i]]
+            for h in range(2):
+                out_ref[i, h * HALF : (h + 1) * HALF, columns] = whole[:, h * width : (h + 1) * width]
 
     for c in range(CHUNKS):
         columns = slice(c * width, (c + 1) * width)
@@ -181,7 +206,10 @@
             def _(i):
                 part = edge_in[c, side, i].astype(jnp.int32).astype(jnp.float32) * scale_in[c, side, i]
                 spot = i + (0 if side == 0 else TB - EB)
-                out_ref[spot, :, columns] = out_ref[spot, :, columns] + part
+                for h in range(2):
+                    lines = slice(h * HALF, (h + 1) * HALF)
+                    extra = part[:, h * width : (h + 1) * width]
+                    out_ref[spot, lines, columns] = out_ref[spot, lines, columns] + extra
 
     for c in range(CHUNKS):
         for k in ORDER:
@@ -215,16 +243,17 @@
             pltpu.VMEM(tile_target.shape, jnp.int32),
             pltpu.VMEM((blocks, BLOCK, COLS), jnp.bfloat16),
             pltpu.VMEM((count, BLOCK * BLOCK), jnp.bfloat16),
-            pltpu.VMEM((count, BLOCK, 2 * BLOCK), jnp.float32),
+            pltpu.VMEM((count, HALF, 2 * BLOCK), jnp.float32),
             pltpu.VMEM((CHUNKS, size, cap, BLOCK, width), jnp.bfloat16),
             pltpu.VMEM((CHUNKS, size * cap, BLOCK, width), jnp.bfloat16),
-            pltpu.VMEM((count, BLOCK, width), jnp.float32),
+            pltpu.VMEM((size * cap, 2 * BLOCK, 2 * width), jnp.bfloat16),
+            pltpu.VMEM((CHUNKS, count, HALF, 2 * width), jnp.float32),
             pltpu.VMEM((8, count), jnp.int32),
             pltpu.SMEM((8, count), jnp.int32),
-            pltpu.VMEM((CHUNKS, 2, EB, BLOCK, width), jnp.int16),
-            pltpu.VMEM((CHUNKS, 2, EB, 1, width), jnp.float32),
-            pltpu.VMEM((CHUNKS, 2, EB, BLOCK, width), jnp.int16),
-            pltpu.VMEM((CHUNKS, 2, EB, 1, width), jnp.float32),
+            pltpu.VMEM((CHUNKS, 2, EB, HALF, 2 * width), jnp.int16),
+            pltpu.VMEM((CHUNKS, 2, EB, 1, 2 * width), jnp.float32),
+            pltpu.VMEM((CHUNKS, 2, EB, HALF, 2 * width), jnp.int16),
+            pltpu.VMEM((CHUNKS, 2, EB, 1, 2 * width), jnp.float32),
             dma((7,)),
             dma((CHUNKS, size)),
             dma((CHUNKS, size)),

time: 37.2 us -> 37.1 us (level)
  no operation moved by 1% of the time
where the time goes in v3:
time: 37.1 us; the launch traced here: 37 us
  Pallas kernels  35.7 us (96%)
  local copies, waits for them, and re-layouts  1.32 us (4%)
    pallas_call x1, Pallas kernels, body(): pl.pallas_call(functools.partial(kernel, groups, size), out_shape=jax.Sha...  35.7 us
    unnamed x1, local copies, waits for them, and re-layouts  1.32 us

profile of v3, /device:TPU:1, one launch (start us, length us, event | category | flops | bytes accessed | tf_op | source)
XLA Modules:
  0.0 37.0 jit_solution(11624152391905037483)
XLA Ops:
  0.0 35.7 %shard_map.64 = f32[32,64,256]{2,1,0:T(8,128)S(1)} custom-call(s32[1,16]{1,0:T(1,128)} %ids_hbm.1, s32[1,8]{1,0:T(1,128)} %counts_hbm.1, s32[1,128]{1,0:T(1,128)} %slot_hbm.1, s32[1,128]{1,0:T(1,128)} %target_hbm.1, bf16[16,64,256]{2,1,0:T(8,128)(2,1)} %bitcast.3, bf16[128,4096]{1,0:T(8,128)(2,1)} %weights_hbm.1), custom_call_target="tpu_custom_call" | custom-call | tf_op jit(solution)/shard_map/pallas_call | solution.py:234
  35.7 1.3 %copy.8 = f32[2048,256]{1,0:T(8,128)} copy(f32[2048,256]{1,0:T(8,128)S(1)} %bitcast.2) | data formatting | bytes 4194304

commit v4 on v3

--- a/solution.py
+++ b/solution.py
@@ -49,7 +49,7 @@
     ids_hbm, counts_hbm, slot_hbm, target_hbm, source_hbm, weights_hbm, out_ref,
     ids_ref, counts_ref, slot_ref, target_ref, source, flat, tiles, outgoing, received, twice, sums, table, table_s,
     edge_out, scale_out, edge_in, scale_in,
-    local_sem, send_sem, recv_sem, edge_send, edge_recv,
+    local_sem, send_sem, recv_sem, edge_send, edge_recv, ready,
 ):
     group, me = lax.axis_index("grp"), lax.axis_index("blk")
     count = slot_hbm.shape[1]
@@ -59,10 +59,21 @@
     before = ((group + groups - 1 + (me + size - 1) // size) % groups, (me + size - 1) % size)
 
     barrier = pltpu.get_barrier_semaphore()
+    outer = (me == 0) | (me == size - 1)
     for k in range(1, size):
-        pl.semaphore_signal(barrier, inc=1, device_id=(group, (me + k) % size), device_id_type=MESH)
-    pl.semaphore_signal(barrier, inc=1, device_id=after, device_id_type=MESH)
-    pl.semaphore_signal(barrier, inc=1, device_id=before, device_id_type=MESH)
+        peer = (me + k) % size
+
+        @pl.when((peer != 0) & (peer != size - 1))
+        def _():
+            pl.semaphore_signal(barrier, inc=1, device_id=(group, peer), device_id_type=MESH)
+
+    @pl.when(me == 0)
+    def _():
+        pl.semaphore_signal(barrier, inc=1, device_id=before, device_id_type=MESH)
+
+    @pl.when(me == size - 1)
+    def _():
+        pl.semaphore_signal(barrier, inc=1, device_id=after, device_id_type=MESH)
 
     pairs = (
         (ids_hbm, ids_ref), (counts_hbm, counts_ref), (source_hbm, source),
@@ -103,7 +114,23 @@
         return copies
 
     pack(0)
-    pl.semaphore_wait(barrier, size + 1)
+
+    @pl.when(jnp.logical_not(outer))
+    def _():
+        pl.semaphore_wait(barrier, size - 1)
+
+    @pl.when(me == 1)
+    def _():
+        pl.semaphore_signal(ready, inc=1, device_id=(group, 0), device_id_type=MESH)
+
+    @pl.when(me == size - 2)
+    def _():
+        pl.semaphore_signal(ready, inc=1, device_id=(group, size - 1), device_id_type=MESH)
+
+    @pl.when(outer)
+    def _():
+        pl.semaphore_wait(ready, 1)
+
     sends = [send(0)]
     pack(1)
 
@@ -171,6 +198,12 @@
             return total
 
         lax.fori_loop(0, count // UNROLL, run, jnp.zeros((HALF, 2 * width), jnp.float32))
+
+        if c == 0:
+
+            @pl.when(outer)
+            def _():
+                pl.semaphore_wait(barrier, 1)
 
         edges.append({})
         for piece, side in PIECES:
@@ -259,6 +292,7 @@
             dma((CHUNKS, size)),
             dma((CHUNKS, 2, EB // PIECE, 2)),
             dma((CHUNKS, 2, EB // PIECE, 2)),
+            pltpu.SemaphoreType.REGULAR,
         ],
         compiler_params=pltpu.CompilerParams(
             collective_id=0, has_side_effects=True, vmem_limit_bytes=48 << 20

time: 37.1 us -> 36.5 us (0.984)
  the two profiles are of different devices: /device:TPU:1 before, /device:TPU:8 now
where the time goes in v4:
time: 36.5 us; the launch traced here: 36.3 us
  Pallas kernels  35 us (96%)
  local copies, waits for them, and re-layouts  1.32 us (4%)
    pallas_call x1, Pallas kernels, body(): pl.pallas_call(functools.partial(kernel, groups, size), out_shape=jax.Sha...  35 us
    unnamed x1, local copies, waits for them, and re-layouts  1.32 us

profile of v4, /device:TPU:8, one launch (start us, length us, event | category | flops | bytes accessed | tf_op | source)
XLA Modules:
  0.0 36.3 jit_solution(15701718200675596545)
XLA Ops:
  0.0 35.0 %shard_map.64 = f32[32,64,256]{2,1,0:T(8,128)S(1)} custom-call(s32[1,16]{1,0:T(1,128)} %ids_hbm.1, s32[1,8]{1,0:T(1,128)} %counts_hbm.1, s32[1,128]{1,0:T(1,128)} %slot_hbm.1, s32[1,128]{1,0:T(1,128)} %target_hbm.1, bf16[16,64,256]{2,1,0:T(8,128)(2,1)} %bitcast.3, bf16[128,4096]{1,0:T(8,128)(2,1)} %weights_hbm.1), custom_call_target="tpu_custom_call" | custom-call | tf_op jit(solution)/shard_map/pallas_call | solution.py:267
  35.0 1.3 %copy.8 = f32[2048,256]{1,0:T(8,128)} copy(f32[2048,256]{1,0:T(8,128)S(1)} %bitcast.2) | data formatting | bytes 4194304

commit v5 on v4

--- a/solution.py
+++ b/solution.py
@@ -67,14 +67,6 @@
         def _():
             pl.semaphore_signal(barrier, inc=1, device_id=(group, peer), device_id_type=MESH)
 
-    @pl.when(me == 0)
-    def _():
-        pl.semaphore_signal(barrier, inc=1, device_id=before, device_id_type=MESH)
-
-    @pl.when(me == size - 1)
-    def _():
-        pl.semaphore_signal(barrier, inc=1, device_id=after, device_id_type=MESH)
-
     pairs = (
         (ids_hbm, ids_ref), (counts_hbm, counts_ref), (source_hbm, source),
         (slot_hbm, slot_ref), (target_hbm, target_ref), (weights_hbm, flat),
@@ -182,6 +174,16 @@
         for k in ORDER:
             sends[c][k].wait_recv()
 
+        if c == 0:
+
+            @pl.when(me == 0)
+            def _():
+                pl.semaphore_signal(barrier, inc=1, device_id=before, device_id_type=MESH)
+
+            @pl.when(me == size - 1)
+            def _():
+                pl.semaphore_signal(barrier, inc=1, device_id=after, device_id_type=MESH)
+
         @pl.loop(0, size * cap)
         def _(slot):
             block = received[c, slot]
@@ -201,7 +203,7 @@
 
         if c == 0:
 
-            @pl.when(outer)
+            @pl.when(me == size - 1)
             def _():
                 pl.semaphore_wait(barrier, 1)
 
@@ -217,8 +219,19 @@
                 scale_out[c, side, i] = most * (1.0 / STEPS)
 
             edges[c][piece, side] = edge_copies(c, side, piece)
-            for copy in edges[c][piece, side]:
-                copy.start()
+
+            @pl.when((side == 0) | (me != 0))
+            def _():
+                for copy in edges[c][piece, side]:
+                    copy.start()
+
+    @pl.when(me == 0)
+    def _():
+        pl.semaphore_wait(barrier, 1)
+        for c in range(CHUNKS):
+            for piece in range(EB // PIECE):
+                for copy in edges[c][piece, 1]:
+                    copy.start()
 
     for c in range(CHUNKS):
         columns = slice(c * width, (c + 1) * width)

time: 36.5 us -> 29.7 us (0.81)
  the two profiles are of different devices: /device:TPU:8 before, /device:TPU:1 now
where the time goes in v5:
time: 29.7 us; the launch traced here: 29.5 us
  Pallas kernels  28.2 us (95%)
  local copies, waits for them, and re-layouts  1.32 us (4%)
    pallas_call x1, Pallas kernels, body(): pl.pallas_call(functools.partial(kernel, groups, size), out_shape=jax.Sha...  28.2 us
    unnamed x1, local copies, waits for them, and re-layouts  1.32 us

profile of v5, /device:TPU:1, one launch (start us, length us, event | category | flops | bytes accessed | tf_op | source)
XLA Modules:
  0.0 29.5 jit_solution(13822239431261257310)
XLA Ops:
  0.0 28.2 %shard_map.64 = f32[32,64,256]{2,1,0:T(8,128)S(1)} custom-call(s32[1,16]{1,0:T(1,128)} %ids_hbm.1, s32[1,8]{1,0:T(1,128)} %counts_hbm.1, s32[1,128]{1,0:T(1,128)} %slot_hbm.1, s32[1,128]{1,0:T(1,128)} %target_hbm.1, bf16[16,64,256]{2,1,0:T(8,128)(2,1)} %bitcast.3, bf16[128,4096]{1,0:T(8,128)(2,1)} %weights_hbm.1), custom_call_target="tpu_custom_call" | custom-call | tf_op jit(solution)/shard_map/pallas_call | solution.py:280
  28.2 1.3 %copy.8 = f32[2048,256]{1,0:T(8,128)} copy(f32[2048,256]{1,0:T(8,128)S(1)} %bitcast.2) | data formatting | bytes 4194304

commit v6 on v5

--- a/solution.py
+++ b/solution.py
@@ -14,7 +14,7 @@
 EB = 16
 SEG = TB + 2 * EB
 CHUNKS = 2
-UNROLL = 32
+UNROLL = 64
 ORDER = (4, 3, 5, 2, 6, 1, 7)
 STEPS = 32766.0
 PIECE = 4
@@ -184,7 +184,7 @@
             def _():
                 pl.semaphore_signal(barrier, inc=1, device_id=after, device_id_type=MESH)
 
-        @pl.loop(0, size * cap)
+        @pl.loop(0, size * cap, unroll=4)
         def _(slot):
             block = received[c, slot]
             twice[slot, :BLOCK, :width] = block
@@ -210,7 +210,7 @@
         edges.append({})
         for piece, side in PIECES:
 
-            @pl.loop(piece * PIECE, (piece + 1) * PIECE)
+            @pl.loop(piece * PIECE, (piece + 1) * PIECE, unroll=True)
             def _(i):
                 whole = sums[c, table_s[3, side * EB + i]]
                 most = jnp.maximum(jnp.max(jnp.abs(whole), axis=0, keepdims=True), 1e-30)
@@ -248,7 +248,7 @@
             for copy in edges[c][piece, side]:
                 copy.wait_recv()
 
-            @pl.loop(piece * PIECE, (piece + 1) * PIECE)
+            @pl.loop(piece * PIECE, (piece + 1) * PIECE, unroll=True)
             def _(i):
                 part = edge_in[c, side, i].astype(jnp.int32).astype(jnp.float32) * scale_in[c, side, i]
                 spot = i + (0 if side == 0 else TB - EB)

time: 29.7 us -> 29.2 us (0.983)
  Pallas kernels: 28.2 us -> 27.7 us
    pallas_call x1, Pallas kernels: 28.2 us -> 27.7 us  [body(): pl.pallas_call(functools.partial(kernel, groups, size), out_shape=jax.Sha...]
where the time goes in v6:
time: 29.2 us; the launch traced here: 29.1 us
  Pallas kernels  27.7 us (95%)
  local copies, waits for them, and re-layouts  1.32 us (5%)
    pallas_call x1, Pallas kernels, body(): pl.pallas_call(functools.partial(kernel, groups, size), out_shape=jax.Sha...  27.7 us
    unnamed x1, local copies, waits for them, and re-layouts  1.32 us

profile of v6, /device:TPU:1, one launch (start us, length us, event | category | flops | bytes accessed | tf_op | source)
XLA Modules:
  0.0 29.1 jit_solution(14718967282369265272)
XLA Ops:
  0.0 27.7 %shard_map.64 = f32[32,64,256]{2,1,0:T(8,128)S(1)} custom-call(s32[1,16]{1,0:T(1,128)} %ids_hbm.1, s32[1,8]{1,0:T(1,128)} %counts_hbm.1, s32[1,128]{1,0:T(1,128)} %slot_hbm.1, s32[1,128]{1,0:T(1,128)} %target_hbm.1, bf16[16,64,256]{2,1,0:T(8,128)(2,1)} %bitcast.3, bf16[128,4096]{1,0:T(8,128)(2,1)} %weights_hbm.1), custom_call_target="tpu_custom_call" | custom-call | tf_op jit(solution)/shard_map/pallas_call | solution.py:280
  27.7 1.3 %copy.8 = f32[2048,256]{1,0:T(8,128)} copy(f32[2048,256]{1,0:T(8,128)S(1)} %bitcast.2) | data formatting | bytes 4194304
